TPU v7x, 32 devices: a whole 2x2x4 slice. The times are simulated.
32 devices in a mesh: dp: 8 (over z, y), tensor: 4 (over x, core).
Axes of the slice: x: 2, y: 2, z: 4, core: 2. Of those that a mesh axis runs over, the one named last changes fastest.
Arguments:
- layer_input: bfloat16 [16384, 1024], P('dp'), may hold values from -6 to 6
- positions: int32 [16384], P('dp'), may hold values from 0 to 2047, as said below
- block_ids: int32 [16384], P('dp'), may hold values from 0 to 31, as said below
- ln_gain: float32 [1024], replicated, may hold values from 0.5 to 1.5
- ln_bias: float32 [1024], replicated, may hold values from -1 to 1
- w_qkv: bfloat16 [1024, 3072], P(None, 'tensor'), may hold values from -0.1875 to 0.1875
- b_qkv: float32 [3072], P('tensor'), may hold values from -1 to 1
- w_dense: bfloat16 [1024, 1024], P('tensor'), may hold values from -0.75 to 0.75
- b_dense: float32 [1024], replicated, may hold values from -1 to 1
- w_in: bfloat16 [1024, 4096], P(None, 'tensor'), may hold values from -0.1875 to 0.1875
- b_in: float32 [4096], P('tensor'), may hold values from -1 to 1
- w_out: bfloat16 [4096, 1024], P('tensor'), may hold values from -0.09375 to 0.09375
- b_out: float32 [1024], replicated, may hold values from -1 to 1
- cotangent: bfloat16 [16384, 1024], P('dp'), may hold values from -6 to 6
Outputs:
- output: bfloat16 [16384, 1024], P('dp')
- grad_input: float32 [16384, 1024], P('dp')
- grad_ln_gain: float32 [1024], replicated
- grad_ln_bias: float32 [1024], replicated
- grad_w_qkv: float32 [1024, 3072], P(None, 'tensor')
- grad_b_qkv: float32 [3072], P('tensor')
- grad_w_dense: float32 [1024, 1024], P('tensor')
- grad_b_dense: float32 [1024], replicated
- grad_w_in: float32 [1024, 4096], P(None, 'tensor')
- grad_b_in: float32 [4096], P('tensor')
- grad_w_out: float32 [4096, 1024], P('tensor')
- grad_b_out: float32 [1024], replicated
Inputs may be any that keep to these rules, and one draw needn't show every extreme that they name: Each sequence of 2048 tokens packs up to four documents: positions rise by one from token to token and return to 0 where a document starts. The first sequence is one document. block_ids = (s + t) // 256 for the t-th token of a sequence, with an offset s of 0 to 6144 for each sequence, 0 for the first and 6144 for the last.
All inputs are finite; a program needn't handle non-finite values.
Results may differ from a plain program's by a relative error of at most 0.008.
Values sent between devices are 32-bit elements; how exact they have to be, the bound alone decides.
A program may use at most 192 MiB of HBM per device.

v0:
```python
import jax
import jax.numpy as jnp
from jax import lax
from jax.sharding import PartitionSpec as P

HD = 64
ROT = 16
QBLOCK = 512


eps = 1e-05
rotary_base = 10000.0


def angles(positions):
    frequency = rotary_base ** (-jnp.arange(0, ROT, 2).astype(jnp.float32) / ROT)
    phases = positions.astype(jnp.float32)[:, None] * frequency[None, :]
    phases = jnp.concatenate([phases, phases], axis=-1)
    return (jnp.cos(phases)[:, None, :], jnp.sin(phases)[:, None, :])


def rotate(source, cosine, sine_part):
    half_rot = ROT // 2
    rot_part = source[..., :ROT]
    turned = jnp.concatenate([-rot_part[..., half_rot:], rot_part[..., :half_rot]], axis=-1)
    return jnp.concatenate([rot_part * cosine + turned * sine_part, source[..., ROT:]], axis=-1)


def turn_back(grad_rot, cosine, sine_part):
    half_rot = ROT // 2
    rot_part = grad_rot[..., :ROT]
    sined = rot_part * sine_part
    moved = jnp.concatenate([sined[..., half_rot:], -sined[..., :half_rot]], axis=-1)
    return jnp.concatenate([rot_part * cosine + moved, grad_rot[..., ROT:]], axis=-1)


def norm_back(d_rows, std_rows, inv_rows, cot_rows, gain):
    grad_gain = jnp.sum(d_rows * std_rows, axis=0)
    grad_shift = jnp.sum(d_rows, axis=0)
    scaled = d_rows * gain
    inner = (
        scaled
        - jnp.mean(scaled, axis=-1, keepdims=True)
        - std_rows * jnp.mean(scaled * std_rows, axis=-1, keepdims=True)
    )
    return (cot_rows + inv_rows * inner, grad_gain, grad_shift)


def on_device(
    layer_input,
    positions,
    block_ids,
    ln_gain,
    ln_bias,
    w_qkv,
    b_qkv,
    w_dense,
    b_dense,
    w_in,
    b_in,
    w_out,
    b_out,
    cotangent,
):
    seq_len = layer_input.shape[0]
    heads_here = w_dense.shape[0] // HD
    input_float = layer_input.astype(jnp.float32)
    row_mean = jnp.mean(input_float, axis=-1, keepdims=True)
    centred = input_float - row_mean
    variance = jnp.mean(centred * centred, axis=-1, keepdims=True)
    inv_std = lax.rsqrt(variance + eps)
    standard = centred * inv_std
    normed = (standard * ln_gain + ln_bias).astype(jnp.bfloat16)
    cosine, sine_part = angles(positions)
    projected = (jnp.dot(normed, w_qkv, preferred_element_type=jnp.float32) + b_qkv).reshape(
        seq_len, heads_here, 3, HD
    )
    query = rotate(projected[:, :, 0], cosine, sine_part).astype(jnp.bfloat16)
    keys = rotate(projected[:, :, 1], cosine, sine_part).astype(jnp.bfloat16)
    values = projected[:, :, 2].astype(jnp.bfloat16)
    score_scale = HD ** (-0.5)
    block_count = seq_len // QBLOCK
    query_blocks = query.reshape(block_count, QBLOCK, heads_here, HD)
    block_rows = block_ids.reshape(block_count, QBLOCK)

    def attend(block_item):
        query_block, block_row = block_item
        scores = (
            jnp.einsum("qhd,khd->hqk", query_block, keys, preferred_element_type=jnp.float32)
            * score_scale
        )
        allowed = block_ids[None, None, :] <= block_row[None, :, None]
        scores = jnp.where(allowed, scores, -1e30)
        row_max = jnp.max(scores, axis=-1, keepdims=True)
        exp_scores = jnp.exp(scores - row_max)
        row_total = jnp.sum(exp_scores, axis=-1, keepdims=True)
        attn_prob = (exp_scores / row_total).astype(jnp.bfloat16)
        mixed_block = jnp.einsum(
            "hqk,khd->qhd", attn_prob, values, preferred_element_type=jnp.float32
        )
        return (mixed_block.astype(jnp.bfloat16), row_max[..., 0] + jnp.log(row_total[..., 0]))

    mixed, log_total = lax.map(attend, (query_blocks, block_rows))
    mixed = mixed.reshape(seq_len, heads_here * HD)
    attn_part = jnp.dot(mixed, w_dense, preferred_element_type=jnp.float32)
    hidden = jnp.dot(normed, w_in, preferred_element_type=jnp.float32) + b_in
    activated = jax.nn.gelu(hidden, approximate=False).astype(jnp.bfloat16)
    mlp_part = jnp.dot(activated, w_out, preferred_element_type=jnp.float32)
    branches = lax.psum(attn_part + mlp_part, "tensor")
    output = (input_float + branches + b_dense + b_out).astype(jnp.bfloat16)
    cot_float = cotangent.astype(jnp.float32)
    bias_grad = jnp.sum(cot_float, axis=0)
    grad_w_out = jnp.einsum("tf,td->fd", activated, cotangent, preferred_element_type=jnp.float32)
    d_activated = jnp.dot(cotangent, w_out.T, preferred_element_type=jnp.float32)
    normal_cdf = 0.5 * (1.0 + lax.erf(hidden * 0.7071067811865476))
    normal_pdf = jnp.exp(-0.5 * hidden * hidden) * 0.3989422804014327
    d_hidden = (d_activated * (normal_cdf + hidden * normal_pdf)).astype(jnp.bfloat16)
    grad_w_in = jnp.einsum("td,tf->df", normed, d_hidden, preferred_element_type=jnp.float32)
    grad_b_in = jnp.sum(d_hidden, axis=0, dtype=jnp.float32)
    d_normed = jnp.dot(d_hidden, w_in.T, preferred_element_type=jnp.float32)
    grad_w_dense = jnp.einsum("tc,td->cd", mixed, cotangent, preferred_element_type=jnp.float32)
    d_mixed = jnp.dot(cotangent, w_dense.T, preferred_element_type=jnp.float32).astype(jnp.bfloat16)
    d_mixed_blocks = d_mixed.reshape(block_count, QBLOCK, heads_here, HD)

    def back_step(running, block_item):
        d_keys, d_values = running
        query_block, block_row, d_out_block, total_block = block_item
        scores = (
            jnp.einsum("qhd,khd->hqk", query_block, keys, preferred_element_type=jnp.float32)
            * score_scale
        )
        allowed = block_ids[None, None, :] <= block_row[None, :, None]
        attn_prob = jnp.where(allowed, jnp.exp(scores - total_block[..., None]), 0.0)
        d_prob = jnp.einsum("qhd,khd->hqk", d_out_block, values, preferred_element_type=jnp.float32)
        row_delta = jnp.sum(attn_prob * d_prob, axis=-1, keepdims=True)
        d_scores = (attn_prob * (d_prob - row_delta)).astype(jnp.bfloat16)
        d_query = (
            jnp.einsum("hqk,khd->qhd", d_scores, keys, preferred_element_type=jnp.float32)
            * score_scale
        )
        d_keys = (
            d_keys
            + jnp.einsum("hqk,qhd->khd", d_scores, query_block, preferred_element_type=jnp.float32)
            * score_scale
        )
        d_values = d_values + jnp.einsum(
            "hqk,qhd->khd",
            attn_prob.astype(jnp.bfloat16),
            d_out_block,
            preferred_element_type=jnp.float32,
        )
        return ((d_keys, d_values), d_query)

    empty = jnp.zeros((seq_len, heads_here, HD), jnp.float32)
    (d_keys, d_values), d_query = lax.scan(
        back_step, (empty, empty), (query_blocks, block_rows, d_mixed_blocks, log_total)
    )
    d_query = turn_back(d_query.reshape(seq_len, heads_here, HD), cosine, sine_part)
    d_keys = turn_back(d_keys, cosine, sine_part)
    d_projected = (
        jnp.stack([d_query, d_keys, d_values], axis=2)
        .reshape(seq_len, heads_here * 3 * HD)
        .astype(jnp.bfloat16)
    )
    grad_w_qkv = jnp.einsum("td,tc->dc", normed, d_projected, preferred_element_type=jnp.float32)
    grad_b_qkv = jnp.sum(d_projected, axis=0, dtype=jnp.float32)
    d_normed = d_normed + jnp.dot(d_projected, w_qkv.T, preferred_element_type=jnp.float32)
    d_full = lax.psum(d_normed, "tensor")
    grad_input, grad_gain, grad_shift = norm_back(d_full, standard, inv_std, cot_float, ln_gain)
    (
        grad_gain,
        grad_shift,
        grad_w_qkv,
        grad_b_qkv,
        grad_w_dense,
        bias_grad,
        grad_w_in,
        grad_b_in,
        grad_w_out,
    ) = lax.psum(
        (
            grad_gain,
            grad_shift,
            grad_w_qkv,
            grad_b_qkv,
            grad_w_dense,
            bias_grad,
            grad_w_in,
            grad_b_in,
            grad_w_out,
        ),
        "dp",
    )
    return (
        output,
        grad_input,
        grad_gain,
        grad_shift,
        grad_w_qkv,
        grad_b_qkv,
        grad_w_dense,
        bias_grad,
        grad_w_in,
        grad_b_in,
        grad_w_out,
        bias_grad,
    )


def solution(mesh):
    in_specs = (
        P("dp", None),
        P("dp"),
        P("dp"),
        P(),
        P(),
        P(None, "tensor"),
        P("tensor"),
        P("tensor", None),
        P(),
        P(None, "tensor"),
        P("tensor"),
        P("tensor", None),
        P(),
        P("dp", None),
    )
    out_specs = (
        P("dp", None),
        P("dp", None),
        P(),
        P(),
        P(None, "tensor"),
        P("tensor"),
        P("tensor", None),
        P(),
        P(None, "tensor"),
        P("tensor"),
        P("tensor", None),
        P(),
    )
    return jax.shard_map(
        on_device, mesh=mesh, in_specs=in_specs, out_specs=out_specs, check_vma=False
    )
```

profile of v0, /device:TPU:0, one launch (start us, length us, event | category | flops | bytes accessed | tf_op | source)
XLA Modules:
  0.0 1179.5 jit_solution(9979110754419625952)
XLA Ops:
  10.3 3.1 fusion.53
  15.7 3.5 convolution_add_fusion.2
  31.1 62.0 %while.27 = (s32[]{:T(128)}, bf16[4,512,4,64]{1,3,2,0:T(8,128)(2,1)}, f32[4,4,512]{2,1,0:T(4,128)S(1)}, s32[2048]{0:T(1024)S(1)}, s32[4,512]{1,0:T(4,128)S(1)}, ...) while((s32[]{:T(128)}, ...), condition=%wide.region_5.6_spmd, body=%wide.region_2.5_spmd.sunk | while | flops 1125251072 | bytes 61422720 | solution.py:103
  31.8 4.4 fusion.141
  36.2 4.3 fusion.142
  40.6 5.9 fusion.143
  47.2 4.4 fusion.141
  51.7 4.3 fusion.142
  56.0 5.9 fusion.143
  62.6 4.4 fusion.141
  67.1 4.3 fusion.142
  71.5 5.9 fusion.143
  78.1 4.4 fusion.141
  82.5 4.3 fusion.142
  86.9 5.9 fusion.143
  93.2 4.6 convolution_convert_fusion
  97.7 4.4 reshape.229
  102.1 4.1 copy.49
  106.2 286.6 %while.28 = (s32[]{:T(128)}, f32[2048,4,64]{0,2,1:T(8,128)}, f32[2048,4,64]{0,2,1:T(8,128)}, f32[4,512,4,64]{1,0,3,2:T(4,128)}, bf16[4,512,4,64]{1,3,2,0:T(8,128...) while((s32[]{:T(128)}, f32[2048,4,64]{0,2,1:T(8,128)}, ...), condition=%wide.region_9.10_spmd.clone, body=%wide.region_7.9_spmd.clone.sunk | while | flops 2751068160 | bytes 191439088 | solution.py:155
  106.2 9.1 fusion.153
  116.1 12.8 %multiply_reduce_fusion.3 = (f32[4,512]{1,0:T(4,128)S(1)}, f32[4,512,2048]{2,1,0:T(8,128)}) fusion(f32[4,512,2048]{2,1,0:T(8,128)} %fusion.153, f32[4,512]{1,0:T(4,128)S(1)} %dynamic-slice_bitcast_fusion.2, pred[512,2048]{1,0:T(8,128)(4,1)S(1)} %broadcast_compare_fusion.5, bf16[2048,4,64]{0,2,1:T(8,128)(2,1)S(1)} %copy-done.7, ...), kind=kOutput, calls=%fused_computation.19.clone.1 | convolution fusion | flops 557840384 | bytes 35930624 | tf_op jit(solution)/shard_map/while/body/eval_jaxpr/qhd,khd->hqk/dot_general | solution.py:134
  128.9 12.1 %multiply_convert_fusion.2 = bf16[4,512,2048]{2,1,0:T(8,128)(2,1)S(1)} fusion(f32[4,512,2048]{2,1,0:T(8,128)} %get-tuple-element.396, f32[4,512,2048]{2,1,0:T(8,128)} %fusion.153, f32[4,512]{1,0:T(4,128)S(1)} %get-tuple-element.397, f32[4,512]{1,0:T(4,128)S(1)} %dynamic-slice_bitcast_fusion.2, pred[512,2048]{1,0:T(8,128)(4,1)S(1)} %broadcast_compare_fusion.5), kind=kLoop, calls=%fused_computation.18.clone.1 | loop fusion | flops 25165824 | bytes 43008000 | tf_op jit(solution)/shard_map/while/body/eval_jaxpr/convert_element_type | solution.py:136
  141.0 3.4 copy-done.1
  148.4 11.1 dynamic_update_slice.20
  159.5 6.5 fusion.154
  166.0 10.9 fusion.155
  176.9 9.1 fusion.153
  186.8 12.8 %multiply_reduce_fusion.3 = (f32[4,512]{1,0:T(4,128)S(1)}, f32[4,512,2048]{2,1,0:T(8,128)}) fusion(f32[4,512,2048]{2,1,0:T(8,128)} %fusion.153, f32[4,512]{1,0:T(4,128)S(1)} %dynamic-slice_bitcast_fusion.2, pred[512,2048]{1,0:T(8,128)(4,1)S(1)} %broadcast_compare_fusion.5, bf16[2048,4,64]{0,2,1:T(8,128)(2,1)S(1)} %copy-done.7, ...), kind=kOutput, calls=%fused_computation.19.clone.1 | convolution fusion | flops 557840384 | bytes 35930624 | tf_op jit(solution)/shard_map/while/body/eval_jaxpr/qhd,khd->hqk/dot_general | solution.py:134
  199.6 12.1 %multiply_convert_fusion.2 = bf16[4,512,2048]{2,1,0:T(8,128)(2,1)S(1)} fusion(f32[4,512,2048]{2,1,0:T(8,128)} %get-tuple-element.396, f32[4,512,2048]{2,1,0:T(8,128)} %fusion.153, f32[4,512]{1,0:T(4,128)S(1)} %get-tuple-element.397, f32[4,512]{1,0:T(4,128)S(1)} %dynamic-slice_bitcast_fusion.2, pred[512,2048]{1,0:T(8,128)(4,1)S(1)} %broadcast_compare_fusion.5), kind=kLoop, calls=%fused_computation.18.clone.1 | loop fusion | flops 25165824 | bytes 43008000 | tf_op jit(solution)/shard_map/while/body/eval_jaxpr/convert_element_type | solution.py:136
  211.7 3.4 copy-done.1
  219.1 11.1 dynamic_update_slice.20
  230.3 7.1 fusion.154
  237.3 11.5 fusion.155
  248.8 9.1 fusion.153
  258.7 12.8 %multiply_reduce_fusion.3 = (f32[4,512]{1,0:T(4,128)S(1)}, f32[4,512,2048]{2,1,0:T(8,128)}) fusion(f32[4,512,2048]{2,1,0:T(8,128)} %fusion.153, f32[4,512]{1,0:T(4,128)S(1)} %dynamic-slice_bitcast_fusion.2, pred[512,2048]{1,0:T(8,128)(4,1)S(1)} %broadcast_compare_fusion.5, bf16[2048,4,64]{0,2,1:T(8,128)(2,1)S(1)} %copy-done.7, ...), kind=kOutput, calls=%fused_computation.19.clone.1 | convolution fusion | flops 557840384 | bytes 35930624 | tf_op jit(solution)/shard_map/while/body/eval_jaxpr/qhd,khd->hqk/dot_general | solution.py:134
  271.5 12.1 %multiply_convert_fusion.2 = bf16[4,512,2048]{2,1,0:T(8,128)(2,1)S(1)} fusion(f32[4,512,2048]{2,1,0:T(8,128)} %get-tuple-element.396, f32[4,512,2048]{2,1,0:T(8,128)} %fusion.153, f32[4,512]{1,0:T(4,128)S(1)} %get-tuple-element.397, f32[4,512]{1,0:T(4,128)S(1)} %dynamic-slice_bitcast_fusion.2, pred[512,2048]{1,0:T(8,128)(4,1)S(1)} %broadcast_compare_fusion.5), kind=kLoop, calls=%fused_computation.18.clone.1 | loop fusion | flops 25165824 | bytes 43008000 | tf_op jit(solution)/shard_map/while/body/eval_jaxpr/convert_element_type | solution.py:136
  283.6 3.4 copy-done.1
  291.0 11.1 dynamic_update_slice.20
  302.2 7.1 fusion.154
  309.2 11.5 fusion.155
  320.7 9.1 fusion.153
  330.6 12.8 %multiply_reduce_fusion.3 = (f32[4,512]{1,0:T(4,128)S(1)}, f32[4,512,2048]{2,1,0:T(8,128)}) fusion(f32[4,512,2048]{2,1,0:T(8,128)} %fusion.153, f32[4,512]{1,0:T(4,128)S(1)} %dynamic-slice_bitcast_fusion.2, pred[512,2048]{1,0:T(8,128)(4,1)S(1)} %broadcast_compare_fusion.5, bf16[2048,4,64]{0,2,1:T(8,128)(2,1)S(1)} %copy-done.7, ...), kind=kOutput, calls=%fused_computation.19.clone.1 | convolution fusion | flops 557840384 | bytes 35930624 | tf_op jit(solution)/shard_map/while/body/eval_jaxpr/qhd,khd->hqk/dot_general | solution.py:134
  343.4 12.1 %multiply_convert_fusion.2 = bf16[4,512,2048]{2,1,0:T(8,128)(2,1)S(1)} fusion(f32[4,512,2048]{2,1,0:T(8,128)} %get-tuple-element.396, f32[4,512,2048]{2,1,0:T(8,128)} %fusion.153, f32[4,512]{1,0:T(4,128)S(1)} %get-tuple-element.397, f32[4,512]{1,0:T(4,128)S(1)} %dynamic-slice_bitcast_fusion.2, pred[512,2048]{1,0:T(8,128)(4,1)S(1)} %broadcast_compare_fusion.5), kind=kLoop, calls=%fused_computation.18.clone.1 | loop fusion | flops 25165824 | bytes 43008000 | tf_op jit(solution)/shard_map/while/body/eval_jaxpr/convert_element_type | solution.py:136
  355.5 3.4 copy-done.1
  362.9 11.1 dynamic_update_slice.20
  374.0 7.1 fusion.154
  381.1 11.5 fusion.155
  392.8 3.7 reshape.228
  408.1 23.0 %fusion.59 = (bf16[2048,1024]{1,0:T(8,128)(2,1)}, f32[2048,1024]{1,0:T(8,128)S(1)}) fusion(f32[1024]{0:T(1024)S(1)} %copy-done.40, bf16[2048,1024]{1,0:T(8,128)(2,1)S(1)} %copy-done.14, bf16[1024,1024]{1,0:T(8,128)(2,1)S(1)} %copy-done), kind=kOutput, calls=%fused_computation.75 | convolution fusion | flops 4433379328 | bytes 18878464 | tf_op jit(solution)/shard_map/dot_general | solution.py:106
  431.1 9.1 convert_reduce_fusion.2
  440.2 6.7 fusion.84
  446.9 4.6 fusion.83
  451.6 6.2 convolution_add_fusion.1
  457.7 4.7 convolution_add_fusion
  462.6 4.4 fusion.86
  467.0 8.5 fusion.85
  475.4 6.3 fusion.87
  481.8 6.1 fusion.88
  488.0 266.2 %all-reduce.8.cloned.1.call-done = (f32[2048,1024]{1,0:T(8,128)}, f32[2048,1024]{1,0:T(8,128)}) async-done(((f32[2048,1024]{1,0:T(8,128)}, f32[2048,1024]{1,0:T(8,128)}), (f32[2048,1024]{1,0:T(8,128)}, f32[2048,1024]{1,0:T(8,128)})) %all-reduce.8.cloned.1.call-update) | async-done | bytes 16777232 | tf_op jit(solution)/shard_map/psum | solution.py:109
  754.2 7.6 fusion.52
  762.5 12.8 %convert_reduce_fusion.1 = (f32[1024]{0:T(1024)S(1)}, f32[2048,1024]{1,0:T(8,128)}, bf16[2048,1024]{1,0:T(8,128)(2,1)}) fusion(bf16[2048,1024]{1,0:T(8,128)(2,1)} %param.31, f32[2048]{0:T(1024)S(1)} %broadcast_multiply_fusion.1, f32[2048]{0:T(1024)S(1)} %copy-done.26, bf16[2048,1024]{1,0:T(8,128)(2,1)S(1)} %copy-done.5, ...), kind=kLoop, calls=%fused_computation.55 | loop fusion | flops 31456256 | bytes 37797888 | tf_op jit(solution)/shard_map/reduce_sum | solution.py:112
  775.3 40.2 %all-reduce = (f32[1024]{0:T(1024)}, f32[1024]{0:T(1024)}, f32[768]{0:T(1024)}, f32[1024]{0:T(1024)S(1)}, f32[1024]{0:T(1024)}) all-reduce(f32[1024]{0:T(1024)S(1)} %get-tuple-element.188, f32[1024]{0:T(1024)S(1)} %get-tuple-element.191, f32[768]{0:T(1024)S(1)} %reduce_sum.108, ...), channel_id=1, replica_groups=mesh['dp'=8,'tensor'=4] {'dp'}, use_global_device_ids=true, to_apply=%region_14.15 | all-reduce | flops 4864 | bytes 38912 | tf_op jit(solution)/shard_map/psum | solution.py:180
  815.5 345.8 %all-reduce.6.cloned.1.call-done = (f32[1024,768]{1,0:T(8,128)}, f32[256,1024]{1,0:T(8,128)}, f32[1024,1024]{1,0:T(8,128)}, f32[1024,1024]{1,0:T(8,128)}) async-done(((f32[1024,768]{1,0:T(8,128)}, f32[256,1024]{1,0:T(8,128)}, f32[1024,1024]{1,0:T(8,128)}, f32[1024,1024]{1,0:T(8,128)}), (f32[1024,768]{1,0:T(8,128)}, f32[256,1024]{1,0:T(8,128)}, f32[1024,1024]{1,0:T(8,128)}, ...) | async-done | bytes 12582928 | tf_op jit(solution)/shard_map/psum | solution.py:180
  1161.8 4.0 copy.114
  (195 shorter events, 57.9 us)
Async XLA Ops:
  7.2 400.8 %copy-start = (bf16[1024,1024]{1,0:T(8,128)(2,1)S(1)}, bf16[1024,1024]{1,0:T(8,128)(2,1)}, u32[]{:S(2)}) copy-start(bf16[1024,1024]{1,0:T(8,128)(2,1)} %param.27) | copy-start | bytes 6291460
  7.2 6.8 copy-start.29
  7.2 6.8 copy-start.32
  7.2 747.0 %all-reduce.8.cloned.1.call-start = ((), (), s32[]{:S(2)}) async-start(), calls=%async_computation.1 | async-start | bytes 33554432 | tf_op jit(solution)/shard_map/psum | solution.py:109
  7.3 6.7 copy-start.4
  7.3 8.4 copy-start.37
  7.3 8.4 copy-start.39
  10.3 3.1 copy-start.25
  13.4 0.6 copy-start.27
  15.7 3.5 copy-start.13
  19.7 5.0 copy-start.31
  19.7 8.1 copy-start.23
  20.2 1.3 copy-start.9
  20.2 2.3 copy-start.10
  25.0 0.6 copy-start.19
  25.0 2.0 copy-start.21
  36.2 4.4 copy-start.6
  51.6 4.4 copy-start.6
  67.1 4.4 copy-start.6
  82.5 4.4 copy-start.6
  106.2 291.8 %copy-start.20 = (f32[2048,16]{0,1:T(8,128)S(1)}, f32[2048,16]{0,1:T(8,128)}, u32[]{:S(2)}) copy-start(f32[2048,16]{0,1:T(8,128)} %copy-done.19) | copy-start | bytes 393220
  106.2 9.8 copy-start.7
  116.0 12.9 %copy-start.2 = (pred[512,2048]{1,0:T(8,128)(4,1)}, pred[512,2048]{1,0:T(8,128)(4,1)S(1)}, u32[]{:S(2)}) copy-start(pred[512,2048]{1,0:T(8,128)(4,1)S(1)} %broadcast_compare_fusion.5) | copy-start | bytes 3145732 | tf_op jit(solution)/shard_map/while
  141.0 3.4 copy-start.1
  159.5 6.5 copy-start.3
  176.9 9.8 copy-start.7
  186.7 12.9 %copy-start.2 = (pred[512,2048]{1,0:T(8,128)(4,1)}, pred[512,2048]{1,0:T(8,128)(4,1)S(1)}, u32[]{:S(2)}) copy-start(pred[512,2048]{1,0:T(8,128)(4,1)S(1)} %broadcast_compare_fusion.5) | copy-start | bytes 3145732 | tf_op jit(solution)/shard_map/while
  211.7 3.4 copy-start.1
  230.3 7.1 copy-start.3
  248.8 9.8 copy-start.7
  258.6 12.9 %copy-start.2 = (pred[512,2048]{1,0:T(8,128)(4,1)}, pred[512,2048]{1,0:T(8,128)(4,1)S(1)}, u32[]{:S(2)}) copy-start(pred[512,2048]{1,0:T(8,128)(4,1)S(1)} %broadcast_compare_fusion.5) | copy-start | bytes 3145732 | tf_op jit(solution)/shard_map/while
  283.6 3.4 copy-start.1
  302.1 7.1 copy-start.3
  320.7 9.8 copy-start.7
  330.5 12.9 %copy-start.2 = (pred[512,2048]{1,0:T(8,128)(4,1)}, pred[512,2048]{1,0:T(8,128)(4,1)S(1)}, u32[]{:S(2)}) copy-start(pred[512,2048]{1,0:T(8,128)(4,1)S(1)} %broadcast_compare_fusion.5) | copy-start | bytes 3145732 | tf_op jit(solution)/shard_map/while
  355.5 3.4 copy-start.1
  374.0 7.1 copy-start.3
  392.8 8.1 copy-start.22
  402.4 5.6 copy-start.14
  402.5 5.6 copy-start.40
  404.9 46.7 %copy-start.18 = (bf16[2048,4,3,64]{0,3,2,1:T(8,128)(2,1)}, bf16[2048,4,3,64]{0,3,2,1:T(8,128)(2,1)S(1)}, u32[]{:S(2)}) copy-start(bf16[2048,4,3,64]{0,3,2,1:T(8,128)(2,1)S(1)} %copy.51) | copy-start | bytes 9437188
  408.0 23.1 %copy-start.11 = (bf16[2048,1024]{1,0:T(8,128)(2,1)S(1)}, bf16[2048,1024]{1,0:T(8,128)(2,1)}, u32[]{:S(2)}) copy-start(bf16[2048,1024]{1,0:T(8,128)(2,1)} %param.31) | copy-start | bytes 12582916
  408.0 23.1 %copy-start.36 = (bf16[1024,1024]{1,0:T(8,128)(2,1)S(1)}, bf16[1024,1024]{1,0:T(8,128)(2,1)}, u32[]{:S(2)}) copy-start(bf16[1024,1024]{1,0:T(8,128)(2,1)} %param.29) | copy-start | bytes 6291460
  440.2 6.7 copy-start.41
  446.9 4.6 copy-start.38
  451.6 6.2 copy-start.24
  462.5 698.7 %all-reduce.6.cloned.1.call-start = ((), (), s32[]{:S(2)}) async-start(), calls=%async_computation | async-start | bytes 25165824 | tf_op jit(solution)/shard_map/psum | solution.py:180
  467.0 8.5 copy-start.15
  467.0 8.5 copy-start.43
  475.4 6.4 copy-start.12
  475.4 6.4 copy-start.42
  487.9 266.3 %copy-start.26 = (f32[2048]{0:T(1024)S(1)}, f32[2048]{0:T(1024)}, u32[]{:S(2)}) copy-start(f32[2048]{0:T(1024)} %copy-done.25) | copy-start | bytes 24580
  487.9 266.3 %copy-start.28 = (f32[2048]{0:T(1024)S(1)}, f32[2048]{0:T(1024)}, u32[]{:S(2)}) copy-start(f32[2048]{0:T(1024)} %copy-done.27) | copy-start | bytes 24580
  487.9 266.3 %copy-start.30 = (f32[1024]{0:T(1024)S(1)}, f32[1024]{0:T(1024)}, u32[]{:S(2)}) copy-start(f32[1024]{0:T(1024)} %param.21) | copy-start | bytes 12292
  487.9 274.0 %copy-start.33 = (f32[1024]{0:T(1024)S(1)}, f32[1024]{0:T(1024)}, u32[]{:S(2)}) copy-start(f32[1024]{0:T(1024)} %param.30) | copy-start | bytes 12292
  487.9 274.0 %copy-start.34 = (f32[1024]{0:T(1024)S(1)}, f32[1024]{0:T(1024)}, u32[]{:S(2)}) copy-start(f32[1024]{0:T(1024)} %param.26) | copy-start | bytes 12292
  754.2 7.7 copy-start.5
  754.2 8.3 copy-start.8
  815.5 354.8 %copy-start.35 = (f32[1024]{0:T(1024)}, f32[1024]{0:T(1024)S(1)}, u32[]{:S(2)}) copy-start(f32[1024]{0:T(1024)S(1)} %get-tuple-element.495) | copy-start | bytes 12292
  1161.2 7.0 copy-start.17
  1161.8 8.4 copy-start.16
Sparse Core Ops, SparseCore 0:
  462.6 291.5 all-reduce.7
  760.1 401.1 all-reduce.5
where the time goes:
time: 1190 us; the launch traced here: 1180 us
  waiting for transfers between devices  612 us (51%)
  matrix products  301 us (25%)
  other arithmetic  107 us (9%)
  local copies, waits for them, and re-layouts  104 us (9%)
  blocking collectives  40.2 us (3%)
  between operations  15.1 us (1%)
    psum x1, waiting for transfers between devices, on_device(): lax.psum((grad_gain, grad_shift, grad_w_qkv, grad_b_qkv, grad_w_dense, bi...  346 us
    psum x1, waiting for transfers between devices, on_device(): branches = lax.psum(attn_part + mlp_part, 'tensor')  266 us
    dot_general x4, matrix products, back_step(): jnp.einsum('qhd,khd->hqk', d_out_block, values, preferred_element_type=jn...  51.3 us
    dynamic_update_slice x8, local copies, waits for them, and re-layouts, on_device(): lax.scan(back_step, (empty, empty), (query_blocks, block_rows, d_mixed_bl...  49.9 us
    convert_element_type x4, other arithmetic, back_step(): d_scores = (attn_prob * (d_prob - row_delta)).astype(jnp.bfloat16)  48.4 us
    dot_general x4, matrix products, back_step(): jnp.einsum('hqk,qhd->khd', attn_prob.astype(jnp.bfloat16), d_out_block, p...  45.4 us
    psum x1, blocking collectives, on_device(): lax.psum((grad_gain, grad_shift, grad_w_qkv, grad_b_qkv, grad_w_dense, bi...  40.2 us
    dot_general x4, matrix products, back_step(): jnp.einsum('qhd,khd->hqk', query_block, keys, preferred_element_type=jnp....  36.5 us
  transfers between devices with their start and end apart: 2, of which 2 were waited for; matrix products, arithmetic and copies ran while one was open for 4% of the time, Pallas kernels for 0%

commit v1 on v0

v1 whole, which is shorter than its diff:
```python
import functools

import jax
import jax.numpy as jnp
import numpy as np
from jax import lax
from jax.experimental import pallas as pl
from jax.experimental.pallas import tpu as pltpu
from jax.sharding import PartitionSpec as P

HD = 64
ROT = 16
TILE = 256

eps = 1e-05
rotary_base = 10000.0
NT = (((1,), (1,)), ((), ()))
TN = (((0,), (0,)), ((), ()))
NN = (((1,), (0,)), ((), ()))


def mm(a, b, dims=NN):
    return lax.dot_general(a, b, dims, preferred_element_type=jnp.float32)


def lane_tables(positions):
    frequency = rotary_base ** (-jnp.arange(0, ROT, 2).astype(jnp.float32) / ROT)
    phases = positions.astype(jnp.float32)[:, None] * frequency[None, :]
    cosine, sine = jnp.cos(phases), jnp.sin(phases)
    tokens = positions.shape[0]
    ones = jnp.ones((tokens, HD - ROT), jnp.float32)
    none = jnp.zeros((tokens, HD - ROT), jnp.float32)
    half = jnp.zeros((tokens, ROT // 2), jnp.float32)
    cos_head = jnp.concatenate([cosine, cosine, ones], axis=1)
    low_head = jnp.concatenate([-sine, half, none], axis=1)
    high_head = jnp.concatenate([half, sine, none], axis=1)
    return tuple(jnp.concatenate([t, t], axis=1) for t in (cos_head, low_head, high_head))


def attention_kernel(
    heads,
    q,
    k,
    v,
    ids_col,
    ids_row,
    cot,
    normed,
    w_dense,
    w_qkv,
    perm,
    cos_t,
    low_t,
    high_t,
    row_mean,
    inv_std,
    x_hbm,
    mlp_hbm,
    dn_hbm,
    out_hbm,
    dnorm_hbm,
    gwd,
    gwqkv,
    gbqkv,
    gln,
    q_t,
    k_t,
    v_t,
    do,
    do_t,
    scores,
    probs,
    dscores,
    stack_a,
    stack_b,
    dk,
    dv,
    dq_t,
    mixed,
    lse,
    delta,
    dproj,
    stage_in,
    stage_x,
    stage_out,
    in_sem,
    x_sem,
    out_sem,
):
    tokens = q.shape[0]
    tiles = tokens // TILE
    width = heads * HD
    lane_head = lax.broadcasted_iota(jnp.int32, (1, width), 1) >> 6

    def head_lanes(h):
        return (lane_head == h).astype(jnp.float32).astype(jnp.bfloat16)

    row_head = lax.broadcasted_iota(jnp.int32, (width, 1), 0) >> 6

    def head_rows(h):
        return (row_head == h).astype(jnp.float32).astype(jnp.bfloat16)

    q_t[...] = q[...].T
    k_t[...] = k[...].T
    v_t[...] = v[...].T
    do[...] = mm(cot[...], w_dense[...], NT).astype(jnp.bfloat16)
    do_t[...] = do[...].T

    def load(hbm, buf, sem, t):
        copy = pltpu.make_async_copy(hbm.at[pl.ds(t * TILE, TILE)], buf, sem)
        copy.start()
        return copy

    def span(i):
        return min(i + 2, tiles) * TILE

    for i in range(tiles):
        fetch = load(mlp_hbm, stage_in, in_sem, i)
        n, cols = span(i), pl.ds(i * TILE, TILE)
        edge = pl.ds(i * TILE, n - i * TILE)

        def head_forward(h, _):
            rows = pl.ds(pl.multiple_of(h * HD, HD), HD)
            scores[0:n] = mm(k[0:n], q_t[:, cols] * head_rows(h))
            allowed = ids_col[edge, :] <= ids_row[:, cols]
            scores[edge] = jnp.where(allowed, scores[edge], -1e30)
            top = jnp.max(scores[0:n], axis=0, keepdims=True)
            weights = jnp.exp(scores[0:n] - top)
            total = jnp.sum(weights, axis=0, keepdims=True)
            probs[0:n, 0:TILE] = weights.astype(jnp.bfloat16)
            head_out = mm(v_t[rows, 0:n], probs[0:n, 0:TILE]) / total
            lse[pl.ds(h, 1), cols] = top + jnp.log(total)
            delta[pl.ds(h, 1), cols] = jnp.sum(
                head_out * do_t[rows, cols].astype(jnp.float32), axis=0, keepdims=True
            )
            dq_t[rows, cols] = head_out
            return 0

        lax.fori_loop(0, heads, head_forward, 0)
        mixed_tile = dq_t[:, cols].T.astype(jnp.bfloat16)
        mixed[cols] = mixed_tile
        if i:
            push.wait()
        fetch.wait()
        stage_out[...] = mm(mixed_tile, w_dense[...]) + stage_in[...]
        push = pltpu.make_async_copy(stage_out, out_hbm.at[cols], out_sem)
        push.start()

    gwd[...] = mm(mixed[...], cot[...], TN)

    def rotate_back(grad, rows):
        halves = []
        for part in range(width // 128):
            g = grad[:, part * 128 : (part + 1) * 128]
            halves.append(
                g * cos_t[rows]
                - pltpu.roll(g, 120, 1) * low_t[rows]
                - pltpu.roll(g, 8, 1) * high_t[rows]
            )
        return jnp.concatenate(halves, axis=1)

    def finish(t, push):
        rows = pl.ds(t * TILE, TILE)
        fetch = load(dn_hbm, stage_in, in_sem, t)
        fetch_x = load(x_hbm, stage_x, x_sem, t)
        dq_tile = rotate_back(dq_t[:, rows].T * (HD**-0.5), rows)
        dk_tile = rotate_back(dk[rows], rows)
        joined = jnp.concatenate([dq_tile, dk_tile, dv[rows]], axis=1).astype(jnp.bfloat16)
        laid = mm(joined, perm[...])
        dproj[rows] = laid.astype(jnp.bfloat16)
        gbqkv[...] += jnp.sum(laid, axis=0, keepdims=True)
        push.wait()
        fetch.wait()
        d_tile = mm(dproj[rows], w_qkv[...], NT) + stage_in[...]
        stage_out[...] = d_tile
        push = pltpu.make_async_copy(stage_out, dnorm_hbm.at[rows], out_sem)
        push.start()
        fetch_x.wait()
        standard = (stage_x[...].astype(jnp.float32) - row_mean[rows]) * inv_std[rows]
        gln[0:1] += jnp.sum(d_tile * standard, axis=0, keepdims=True)
        gln[1:2] += jnp.sum(d_tile, axis=0, keepdims=True)
        return push

    gbqkv[...] = jnp.zeros_like(gbqkv)
    gln[...] = jnp.zeros_like(gln)
    for i in reversed(range(tiles)):
        n, cols = span(i), pl.ds(i * TILE, TILE)
        edge = pl.ds(i * TILE, n - i * TILE)
        for h in range(heads):
            stack_a[h * TILE : (h + 1) * TILE] = do[cols] * head_lanes(h)
            stack_b[h * TILE : (h + 1) * TILE] = q[cols] * head_lanes(h)

        def head_backward(h, _):
            rows = pl.ds(pl.multiple_of(h * HD, HD), HD)
            block = pl.ds(pl.multiple_of(h * TILE, TILE), TILE)
            scores[0:n] = mm(k[0:n], q_t[:, cols] * head_rows(h))
            allowed = ids_col[edge, :] <= ids_row[:, cols]
            scores[edge] = jnp.where(allowed, scores[edge], -1e30)
            weights = jnp.exp(scores[0:n] - lse[pl.ds(h, 1), cols])
            probs[0:n, block] = weights.astype(jnp.bfloat16)
            d_weights = mm(v[0:n], do_t[:, cols] * head_rows(h))
            d_tile = weights * (d_weights - delta[pl.ds(h, 1), cols])
            dscores[0:n, block] = d_tile.astype(jnp.bfloat16)
            dq_t[rows, cols] = mm(k_t[rows, 0:n], dscores[0:n, block])
            return 0

        lax.fori_loop(0, heads, head_backward, 0)
        dv_part = mm(probs[0:n], stack_a[...])
        dk_part = mm(dscores[0:n], stack_b[...])
        if i == tiles - 1:
            dv[...] = dv_part
            dk[...] = dk_part
        else:
            dv[0:n] += dv_part
            dk[0:n] += dk_part
        if i < tiles - 1:
            push = finish(i + 1, push)
    push = finish(0, push)
    gwqkv[...] = mm(normed[...], dproj[...], TN)
    push.wait()


def attention(q, k, v, ids, cot, normed, w_dense, w_qkv, tables, row_mean, inv_std, x, mlp, dn):
    tokens, width = q.shape
    heads = width // HD
    d = x.shape[1]
    c = 3 * width
    order = np.arange(c).reshape(3, heads, HD).transpose(1, 0, 2).reshape(-1)
    perm = np.zeros((c, c), np.float32)
    perm[order, np.arange(c)] = 1.0
    vm = pl.BlockSpec(memory_space=pltpu.VMEM)
    hbm = pl.BlockSpec(memory_space=pl.ANY)
    f32, bf16 = jnp.float32, jnp.bfloat16
    scratch = [
        pltpu.VMEM((width, tokens), bf16),
        pltpu.VMEM((width, tokens), bf16),
        pltpu.VMEM((width, tokens), bf16),
        pltpu.VMEM((tokens, width), bf16),
        pltpu.VMEM((width, tokens), bf16),
        pltpu.VMEM((tokens, TILE), f32),
        pltpu.VMEM((tokens, heads * TILE), bf16),
        pltpu.VMEM((tokens, heads * TILE), bf16),
        pltpu.VMEM((heads * TILE, width), bf16),
        pltpu.VMEM((heads * TILE, width), bf16),
        pltpu.VMEM((tokens, width), f32),
        pltpu.VMEM((tokens, width), f32),
        pltpu.VMEM((width, tokens), f32),
        pltpu.VMEM((tokens, width), bf16),
        pltpu.VMEM((8, tokens), f32),
        pltpu.VMEM((8, tokens), f32),
        pltpu.VMEM((tokens, c), bf16),
        pltpu.VMEM((TILE, d), f32),
        pltpu.VMEM((TILE, d), bf16),
        pltpu.VMEM((TILE, d), f32),
        pltpu.SemaphoreType.DMA,
        pltpu.SemaphoreType.DMA,
        pltpu.SemaphoreType.DMA,
    ]
    return pl.pallas_call(
        functools.partial(attention_kernel, heads),
        out_shape=(
            jax.ShapeDtypeStruct((tokens, d), f32),
            jax.ShapeDtypeStruct((tokens, d), f32),
            jax.ShapeDtypeStruct((width, d), f32),
            jax.ShapeDtypeStruct((d, c), f32),
            jax.ShapeDtypeStruct((1, c), f32),
            jax.ShapeDtypeStruct((8, d), f32),
        ),
        in_specs=[vm] * 15 + [hbm] * 3,
        out_specs=(hbm, hbm, vm, vm, vm, vm),
        scratch_shapes=scratch,
        compiler_params=pltpu.CompilerParams(vmem_limit_bytes=60 << 20),
        name="attention",
    )(
        q,
        k,
        v,
        ids[:, None],
        ids[None, :],
        cot,
        normed,
        w_dense,
        w_qkv,
        jnp.asarray(perm, bf16),
        *tables,
        row_mean,
        inv_std,
        x,
        mlp,
        dn,
    )


def rotate(source, tables):
    tokens, width = source.shape
    cos_t, low_t, high_t = tables
    pairs = source.reshape(tokens, width // 128, 128)
    up = jnp.roll(pairs, -8, axis=2)
    down = jnp.roll(pairs, 8, axis=2)
    turned = pairs * cos_t[:, None] + up * low_t[:, None] + down * high_t[:, None]
    return turned.reshape(tokens, width)


def norm_back(d_rows, std_rows, inv_rows, cot_rows, gain):
    scaled = d_rows * gain
    inner = (
        scaled
        - jnp.mean(scaled, axis=-1, keepdims=True)
        - std_rows * jnp.mean(scaled * std_rows, axis=-1, keepdims=True)
    )
    return cot_rows + inv_rows * inner


def on_device(
    layer_input,
    positions,
    block_ids,
    ln_gain,
    ln_bias,
    w_qkv,
    b_qkv,
    w_dense,
    b_dense,
    w_in,
    b_in,
    w_out,
    b_out,
    cotangent,
):
    d = layer_input.shape[1]
    width = w_dense.shape[0]
    heads = width // HD
    input_float = layer_input.astype(jnp.float32)
    row_mean = jnp.mean(input_float, axis=-1, keepdims=True)
    centred = input_float - row_mean
    variance = jnp.mean(centred * centred, axis=-1, keepdims=True)
    inv_std = lax.rsqrt(variance + eps)
    standard = centred * inv_std
    normed = (standard * ln_gain + ln_bias).astype(jnp.bfloat16)
    tables = lane_tables(positions)
    w_parts = w_qkv.reshape(d, heads, 3, HD).transpose(2, 0, 1, 3).reshape(3, d, width)
    b_parts = b_qkv.reshape(heads, 3, HD).transpose(1, 0, 2).reshape(3, width)

    def project(part):
        return jnp.dot(normed, w_parts[part], preferred_element_type=jnp.float32) + b_parts[part]

    query = rotate(project(0), tables).astype(jnp.bfloat16) * jnp.bfloat16(HD**-0.5)
    keys = rotate(project(1), tables).astype(jnp.bfloat16)
    values = project(2).astype(jnp.bfloat16)

    hidden = jnp.dot(normed, w_in, preferred_element_type=jnp.float32) + b_in
    normal_cdf = 0.5 * (1.0 + lax.erf(hidden * 0.7071067811865476))
    activated = (hidden * normal_cdf).astype(jnp.bfloat16)
    mlp_part = jnp.dot(activated, w_out, preferred_element_type=jnp.float32)
    cot_float = cotangent.astype(jnp.float32)
    bias_grad = jnp.sum(cot_float, axis=0)
    grad_w_out = jnp.einsum("tf,td->fd", activated, cotangent, preferred_element_type=jnp.float32)
    d_activated = jnp.dot(cotangent, w_out.T, preferred_element_type=jnp.float32)
    normal_pdf = jnp.exp(-0.5 * hidden * hidden) * 0.3989422804014327
    d_hidden = (d_activated * (normal_cdf + hidden * normal_pdf)).astype(jnp.bfloat16)
    grad_w_in = jnp.einsum("td,tf->df", normed, d_hidden, preferred_element_type=jnp.float32)
    grad_b_in = jnp.sum(d_hidden, axis=0, dtype=jnp.float32)
    d_mlp = jnp.dot(d_hidden, w_in.T, preferred_element_type=jnp.float32)

    branch, d_normed, grad_w_dense, grad_w_qkv, grad_b_qkv, grad_ln = attention(
        query,
        keys,
        values,
        block_ids,
        cotangent,
        normed,
        w_dense,
        w_qkv,
        tables,
        row_mean,
        inv_std,
        layer_input,
        mlp_part,
        d_mlp,
    )
    branches, d_full = lax.psum((branch, d_normed), "tensor")
    output = (input_float + branches + b_dense + b_out).astype(jnp.bfloat16)
    grad_input = norm_back(d_full, standard, inv_std, cot_float, ln_gain)
    grad_gain, grad_shift = lax.psum((grad_ln[0], grad_ln[1]), ("dp", "tensor"))
    (
        grad_w_qkv,
        grad_b_qkv,
        grad_w_dense,
        bias_grad,
        grad_w_in,
        grad_b_in,
        grad_w_out,
    ) = lax.psum(
        (
            grad_w_qkv,
            grad_b_qkv[0],
            grad_w_dense,
            bias_grad,
            grad_w_in,
            grad_b_in,
            grad_w_out,
        ),
        "dp",
    )
    return (
        output,
        grad_input,
        grad_gain,
        grad_shift,
        grad_w_qkv,
        grad_b_qkv,
        grad_w_dense,
        bias_grad,
        grad_w_in,
        grad_b_in,
        grad_w_out,
        bias_grad,
    )


def solution(mesh):
    in_specs = (
        P("dp", None),
        P("dp"),
        P("dp"),
        P(),
        P(),
        P(None, "tensor"),
        P("tensor"),
        P("tensor", None),
        P(),
        P(None, "tensor"),
        P("tensor"),
        P("tensor", None),
        P(),
        P("dp", None),
    )
    out_specs = (
        P("dp", None),
        P("dp", None),
        P(),
        P(),
        P(None, "tensor"),
        P("tensor"),
        P("tensor", None),
        P(),
        P(None, "tensor"),
        P("tensor"),
        P("tensor", None),
        P(),
    )
    return jax.shard_map(
        on_device, mesh=mesh, in_specs=in_specs, out_specs=out_specs, check_vma=False
    )
```

time: 1190 us -> 966 us (0.81)
  matrix products: 301 us -> 57.3 us
  Pallas kernels: 0 us -> 104 us
  other arithmetic: 107 us -> 48.7 us
  blocking collectives: 40.2 us -> 82.8 us
  local copies, waits for them, and re-layouts: 104 us -> 69.9 us
  waiting for transfers between devices: 612 us -> 578 us
    dot_general x35 -> x4, matrix products: 252 us -> 19.3 us  [the longest x3 12.3 us: project(): jnp.dot(normed, w_parts[part], preferred_element_type=jnp.float32)]
    pallas_call x0 -> x1, Pallas kernels: none -> 104 us  [attention(): pl.pallas_call(functools.partial(attention_kernel, heads), out_shape=(jax...]
    dynamic_update_slice x8 -> x0, local copies, waits for them, and re-layouts: 49.9 us -> none  [on_device(): lax.scan(back_step, (empty, empty), (query_blocks, block_rows, d_mixed_bl...]
    convert_element_type x5 -> x2, other arithmetic: 48.4 us -> 1.81 us  [the longest x1 1.81 us: on_device(): keys = rotate(project(1), tables).astype(jnp.bfloat16)]
    psum x1 -> x2, blocking collectives: 40.2 us -> 82.8 us  [the longest x1 43.2 us: on_device(): grad_gain, grad_shift = lax.psum((grad_ln[0], grad_ln[1]), ('dp', 'tensor'))]
    psum x2, waiting for transfers between devices: 612 us -> 578 us  [the longest x1 346 us: on_device(): lax.psum((grad_w_qkv, grad_b_qkv[0], grad_w_dense, bias_grad, grad_w_in,...]
    reduce_sum x6 -> x1, other arithmetic: 27 us -> 6.95 us  [norm_back(): jnp.mean(scaled, axis=-1, keepdims=True)]
    slice x5 -> x7, local copies, waits for them, and re-layouts: 5.48 us -> 22.1 us  [the longest x4 18.9 us: rotate(): up = jnp.roll(pairs, -8, axis=2)]
where the time goes in v1:
time: 966 us; the launch traced here: 956 us
  waiting for transfers between devices  578 us (60%)
  Pallas kernels  104 us (11%)
  blocking collectives  82.8 us (9%)
  local copies, waits for them, and re-layouts  69.9 us (7%)
  matrix products  57.3 us (6%)
  other arithmetic  48.7 us (5%)
  between operations  14.8 us (2%)
    psum x1, waiting for transfers between devices, on_device(): lax.psum((grad_w_qkv, grad_b_qkv[0], grad_w_dense, bias_grad, grad_w_in,...  346 us
    psum x1, waiting for transfers between devices, on_device(): branches, d_full = lax.psum((branch, d_normed), 'tensor')  232 us
    pallas_call x1, Pallas kernels, attention(): pl.pallas_call(functools.partial(attention_kernel, heads), out_shape=(jax...  104 us
    psum x1, blocking collectives, on_device(): grad_gain, grad_shift = lax.psum((grad_ln[0], grad_ln[1]), ('dp', 'tensor'))  43.2 us
    psum x1, blocking collectives, on_device(): lax.psum((grad_w_qkv, grad_b_qkv[0], grad_w_dense, bias_grad, grad_w_in,...  39.6 us
  transfers between devices with their start and end apart: 2, of which 2 were waited for; matrix products, arithmetic and copies ran while one was open for 4% of the time, Pallas kernels for 0%

profile of v1, /device:TPU:0, one launch (start us, length us, event | category | flops | bytes accessed | tf_op | source)
XLA Modules:
  0.0 956.0 jit_solution(8531940596706001725)
XLA Ops:
  7.2 0.0 copy-start
  7.2 0.0 all-reduce.9.cloned.1.call-start
  7.3 0.9 reshape.123
  8.2 0.1 add.140
  8.3 3.0 convert_reduce_fusion
  11.2 0.5 copy-done.2
  11.7 1.4 fusion.10
  13.1 0.0 copy-start.24
  13.1 2.6 copy.35
  15.7 2.3 fusion.29
  18.0 3.3 fusion.6.normed
  21.3 2.0 copy-done.9
  23.3 2.7 convolution_add_fusion.1
  26.0 3.2 reshape.125
  29.2 5.8 fusion.26
  35.0 3.6 fusion.25
  38.7 0.1 add.135
  38.7 4.9 convolution_add_fusion.2
  43.6 3.2 reshape.124
  46.9 5.8 fusion.28
  52.7 3.7 fusion.27
  56.4 0.1 add.145
  56.4 1.4 copy.41.inv_std
  57.8 1.4 copy.40.row_mean
  59.2 1.3 copy.39.ids_col
  60.5 5.5 multiply_cosine_fusion
  66.0 1.0 broadcast_in_dim.12
  67.1 1.0 broadcast_in_dim.11
  68.1 5.4 concatenate.31.low_t
  73.5 5.4 concatenate.33.high_t
  79.0 7.2 multiply_convert_fusion
  86.3 7.9 convert_reduce_fusion.2
  94.1 7.0 fusion.32.dn_hbm
  101.2 6.7 fusion.31.mlp_hbm
  107.8 0.1 broadcast_in_dim.10
  107.9 3.0 concatenate.29.cos_t
  110.9 4.8 fusion.20.v
  115.7 0.3 copy-done.17
  116.0 12.1 %maximum_multiply_fusion.2 = (f32[2048,2,128]{2,1,0:T(2,128)S(1)}, f32[2048,2,128]{2,1,0:T(2,128)S(1)}, f32[2048,2,128]{2,1,0:T(2,128)S(1)}, f32[2048,2,128]{2,1,0:T(2,128)S(1)}) fusion(f32[2048,2,8]{2,1,0:T(2,128)S(1)} %copy-done.15, f32[2048,2,120]{2,1,0:T(2,128)S(1)} %copy-done.17, f32[2048,128]{1,0:T(8,128)S(1)} %copy-done.11, ...), kind=kLoop, calls=%fused_computation.44 | loop fusion | flops 4194304 | bytes 18874368 | tf_op jit(solution)/shard_map/mul | solution.py:300
  128.2 1.0 mul.175
  129.1 0.6 copy-done.13
  129.7 1.8 fusion.21.k
  131.5 1.9 fusion.23.q
  133.4 103.9 %attention.1 = (f32[2048,1024]{1,0:T(8,128)}, f32[2048,1024]{1,0:T(8,128)}, f32[256,1024]{1,0:T(8,128)}, f32[1024,768]{1,0:T(8,128)}, f32[1,768]{1,0:T(1,128)}, /*index=5*/f32[8,1024]{1,0:T(8,128)}) custom-call(bf16[2048,256]{1,0:T(8,128)(2,1)} %fusion.23.q, bf16[2048,256]{1,0:T(8,128)(2,1)} %fusion.21.k, bf16[2048,256]{1,0:T(8,128)(2,1)} %fusion.20.v, ...), custom_call_target="tpu_custom_call" | custom-call | tf_op jit(solution)/shard_map/attention/pallas_call | solution.py:259
  237.4 0.0 all-reduce.9.cloned.1.call-update
  237.4 0.3 all-reduce.7.cloned.1.call-start
  237.7 10.1 %fusion.33 = f32[1024,1024]{1,0:T(8,128)} fusion(bf16[2048,1024]{1,0:T(8,128)(2,1)} %copy-done.9, bf16[2048,1024]{1,0:T(8,128)(2,1)} %copy-done.33), kind=kOutput, calls=%fused_computation.66 | convolution fusion | flops 4294967296 | bytes 12582912 | tf_op jit(solution)/shard_map/td,tf->df/dot_general | solution.py:361
  247.8 6.1 fusion.34
  253.9 0.0 all-reduce.7.cloned.1.call-update
  253.9 0.7 copy-done.28
  254.6 0.8 fusion.30
  255.5 43.2 %all-reduce = (f32[1024]{0:T(1024)}, f32[1024]{0:T(1024)}) all-reduce(f32[1024]{0:T(1024)S(1)} %bitcast.81, f32[1024]{0:T(1024)S(1)} %bitcast.80), channel_id=1, replica_groups=mesh['dp'=8,'tensor'=4] {'dp','tensor'}, use_global_device_ids=true, to_apply=%region_6.7 | all-reduce | flops 2048 | bytes 16384 | tf_op jit(solution)/shard_map/psum | solution.py:384
  298.7 231.8 %all-reduce.9.cloned.1.call-done = (f32[2048,1024]{1,0:T(8,128)}, f32[2048,1024]{1,0:T(8,128)}) async-done(((f32[2048,1024]{1,0:T(8,128)}, f32[2048,1024]{1,0:T(8,128)}), (f32[2048,1024]{1,0:T(8,128)}, f32[2048,1024]{1,0:T(8,128)})) %all-reduce.9.cloned.1.call-update) | async-done | bytes 16777232 | tf_op jit(solution)/shard_map/psum | solution.py:381
  530.5 7.0 multiply_reduce_fusion
  537.5 1.3 copy-done.6
  538.8 12.8 %convert_reduce_fusion.1 = (f32[1024]{0:T(1024)S(1)}, f32[2048,1024]{1,0:T(8,128)}, bf16[2048,1024]{1,0:T(8,128)(2,1)}) fusion(bf16[2048,1024]{1,0:T(8,128)(2,1)} %cot.1, f32[2048]{0:T(1024)S(1)} %broadcast_multiply_fusion, f32[2048]{0:T(1024)S(1)} %broadcast_multiply_fusion.2, bf16[2048,1024]{1,0:T(8,128)(2,1)S(1)} %copy-done.3, ...), kind=kLoop, calls=%fused_computation.4 | loop fusion | flops 31456256 | bytes 37797888 | tf_op jit(solution)/shard_map/reduce_sum | solution.py:356
  551.6 39.6 %all-reduce.1 = (f32[768]{0:T(1024)}, f32[1024]{0:T(1024)S(1)}, f32[1024]{0:T(1024)}) all-reduce(f32[768]{0:T(1024)S(1)} %reduce.3, f32[1024]{0:T(1024)S(1)} %get-tuple-element.40, f32[1024]{0:T(1024)S(1)} %get-tuple-element.65), channel_id=1, replica_groups=mesh['dp'=8,'tensor'=4] {'dp'}, use_global_device_ids=true, to_apply=%region_9.10 | all-reduce | flops 2816 | bytes 22528 | tf_op jit(solution)/shard_map/psum | solution.py:393
  591.2 346.4 %all-reduce.7.cloned.1.call-done = (f32[1024,768]{1,0:T(8,128)}, f32[256,1024]{1,0:T(8,128)}, f32[1024,1024]{1,0:T(8,128)}, f32[1024,1024]{1,0:T(8,128)}) async-done(((f32[1024,768]{1,0:T(8,128)}, f32[256,1024]{1,0:T(8,128)}, f32[1024,1024]{1,0:T(8,128)}, f32[1024,1024]{1,0:T(8,128)}), (f32[1024,768]{1,0:T(8,128)}, f32[256,1024]{1,0:T(8,128)}, f32[1024,1024]{1,0:T(8,128)}, ...) | async-done | bytes 12582928 | tf_op jit(solution)/shard_map/psum | solution.py:393
  937.6 0.6 copy.68
  938.2 3.9 copy.69
  942.1 1.0 copy.70
  943.0 2.1 copy.71
  945.2 1.6 copy-done.18
  946.7 2.0 copy.72
  (67 shorter events, 0.2 us)
Async XLA Ops:
  7.2 71.8 %copy-start = (bf16[1024,1024]{1,0:T(8,128)(2,1)S(1)}, bf16[1024,1024]{1,0:T(8,128)(2,1)}, u32[]{:S(2)}) copy-start(bf16[1024,1024]{1,0:T(8,128)(2,1)} %param.24) | copy-start | bytes 6291460
  7.2 523.3 %all-reduce.9.cloned.1.call-start = ((), (), s32[]{:S(2)}) async-start(), calls=%async_computation.1 | async-start | bytes 33554432 | tf_op jit(solution)/shard_map/psum | solution.py:381
  8.3 3.4 copy-start.2
  13.1 4.9 copy-start.21
  13.1 4.9 copy-start.24
  21.3 2.0 copy-start.9
  29.2 5.8 copy-start.4
  46.9 5.8 copy-start.5
  52.7 3.7 copy-start.23
  52.7 6.5 copy-start.22
  73.5 5.4 copy-start.30
  79.0 7.3 copy-start.7
  79.0 7.3 copy-start.29
  86.2 14.9 %copy-start.31 = (bf16[2048,1024]{1,0:T(8,128)(2,1)}, bf16[2048,1024]{1,0:T(8,128)(2,1)S(1)}, u32[]{:S(2)}) copy-start(bf16[2048,1024]{1,0:T(8,128)(2,1)S(1)} %get-tuple-element.63) | copy-start | bytes 12582916
  94.1 7.0 copy-start.33
  110.9 4.8 copy-start.11
  110.9 4.8 copy-start.12
  110.9 4.8 copy-start.15
  110.9 4.8 copy-start.16
  110.9 5.1 copy-start.17
  116.0 12.1 %copy-start.10 = (f32[2048,128]{1,0:T(8,128)S(1)}, f32[2048,128]{1,0:T(8,128)}, u32[]{:S(2)}) copy-start(f32[2048,128]{1,0:T(8,128)} %concatenate.29.cos_t) | copy-start | bytes 3145732
  128.1 1.6 copy-start.13
  129.7 1.8 copy-start.14
  237.4 700.2 %all-reduce.7.cloned.1.call-start = ((), (), s32[]{:S(2)}) async-start(), calls=%async_computation | async-start | bytes 25165824 | tf_op jit(solution)/shard_map/psum | solution.py:393
  237.7 10.1 %copy-start.8 = (bf16[2048,1024]{1,0:T(8,128)(2,1)S(1)}, bf16[2048,1024]{1,0:T(8,128)(2,1)}, u32[]{:S(2)}) copy-start(bf16[2048,1024]{1,0:T(8,128)(2,1)} %cot.1) | copy-start | bytes 12582916
  237.7 10.1 %copy-start.32 = (bf16[2048,1024]{1,0:T(8,128)(2,1)S(1)}, bf16[2048,1024]{1,0:T(8,128)(2,1)}, u32[]{:S(2)}) copy-start(bf16[2048,1024]{1,0:T(8,128)(2,1)} %copy-done.31) | copy-start | bytes 12582916
  253.9 0.7 copy-start.28
  530.5 7.0 copy-start.3
  530.5 8.3 copy-start.6
  530.5 8.3 copy-start.25
  530.5 8.3 copy-start.26
  591.2 351.8 %copy-start.27 = (f32[1024]{0:T(1024)}, f32[1024]{0:T(1024)S(1)}, u32[]{:S(2)}) copy-start(f32[1024]{0:T(1024)S(1)} %get-tuple-element.100) | copy-start | bytes 12292
  937.6 4.5 copy-start.20
  938.2 4.9 copy-start.19
  943.0 3.7 copy-start.18
  943.0 5.7 copy-start.1
Sparse Core Ops, SparseCore 0:
  237.5 292.9 all-reduce.8
  536.4 401.1 all-reduce.6

commit v2 on v1

--- a/solution.py
+++ b/solution.py
@@ -291,6 +291,299 @@
     )
 
 
+SLOTS = 5
+STAGES = 6
+CHUNK = 64
+MESH_ID = pl.DeviceIdType.MESH
+
+
+def z_stride(group):
+    return 2 if group == 8 else 4
+
+
+class Peers:
+    def __init__(self, dp_size):
+        stride = z_stride(dp_size)
+        d, t = lax.axis_index("dp"), lax.axis_index("tensor")
+        z = lax.rem(lax.div(d, stride), 4)
+        base = d - z * stride
+        self.y_half = lax.rem(d, 2)
+        self.z_half = lax.div(z, 2)
+        self.middle = jnp.logical_or(z == 1, z == 2)
+        self.end = jnp.logical_or(z == 0, z == 3)
+        self.y = (d + 1 - 2 * self.y_half, t)
+        self.z_pair = (base + stride * (z + 1 - 2 * lax.rem(z, 2)), t)
+        self.z_mid = (base + stride * (3 - z), t)
+        self.z_far = (base + stride * lax.rem(z + 2, 4), t)
+        self.core = (d, t + 1 - 2 * lax.rem(t, 2))
+        self.x = (d, lax.rem(t + 2, 4))
+
+    def greet(self):
+        barrier = pltpu.get_barrier_semaphore()
+        partners = (self.y, self.z_pair, self.z_mid, self.z_far, self.core, self.x)
+        for partner in partners:
+            pl.semaphore_signal(barrier, inc=1, device_id=partner, device_id_type=MESH_ID)
+        pl.semaphore_wait(barrier, len(partners))
+
+
+def remote(src, dst, sems, index, device):
+    return pltpu.make_async_remote_copy(
+        src_ref=src,
+        dst_ref=dst,
+        send_sem=sems.at[(0,) + index],
+        recv_sem=sems.at[(1,) + index],
+        device_id=device,
+        device_id_type=MESH_ID,
+    )
+
+
+class LineFirst:
+    def __init__(self, peers, chunks, scratch):
+        self.p, self.chunks = peers, chunks
+        self.land, self.work, self.mid, self.side, self.done, self.sems, self.local = scratch
+
+    @staticmethod
+    def scratch():
+        f32 = jnp.float32
+        return [
+            pltpu.VMEM((SLOTS, CHUNK, 1024), f32),
+            pltpu.VMEM((SLOTS, CHUNK, 1024), f32),
+            pltpu.VMEM((SLOTS, CHUNK // 2, 1024), f32),
+            pltpu.VMEM((SLOTS, CHUNK // 2, 1024), f32),
+            pltpu.VMEM((SLOTS, CHUNK, 1024), f32),
+            pltpu.SemaphoreType.DMA((2, 5, SLOTS)),
+            pltpu.SemaphoreType.DMA((2, SLOTS)),
+        ]
+
+    def stage(self, c, s):
+        p, slot = self.p, c % SLOTS
+        part, total, row, cols = self.chunks[c]
+        rows, lanes = pl.ds(row, CHUNK), pl.ds(0, cols)
+        half = CHUNK // 2
+        own = pl.ds(pl.multiple_of(p.z_half * half, half), half)
+        other = pl.ds(pl.multiple_of((1 - p.z_half) * half, half), half)
+        land, work = self.land.at[slot, :, lanes], self.work.at[slot, :, lanes]
+        mid, side = self.mid.at[slot, :, lanes], self.side.at[slot, :, lanes]
+        done = self.done.at[slot, :, lanes]
+        inward = functools.partial(remote, part.at[rows], land, self.sems, (0, slot), p.z_pair)
+        across = functools.partial(remote, work.at[other], mid, self.sems, (1, slot), p.z_mid)
+        beside = functools.partial(remote, work.at[own], side, self.sems, (2, slot), p.y)
+        back = functools.partial(remote, done.at[own], done.at[own], self.sems, (3, slot), p.z_mid)
+        outward = functools.partial(remote, done, total.at[rows], self.sems, (4, slot), p.z_pair)
+        fetch = functools.partial(pltpu.make_async_copy, part.at[rows], work, self.local.at[0, slot])
+        store = functools.partial(pltpu.make_async_copy, done, total.at[rows], self.local.at[1, slot])
+
+        if s == 0:
+
+            @pl.when(p.end)
+            def _():
+                inward().start()
+
+            @pl.when(p.middle)
+            def _():
+                fetch().start()
+
+        if s == 5:
+
+            @pl.when(p.end)
+            def _():
+                outward().wait_recv()
+                inward().wait_send()
+
+        if s > 0:
+
+            @pl.when(p.middle)
+            def _():
+                if s == 1:
+                    fetch().wait()
+                    inward().wait_recv()
+                    work[...] += land[...]
+                    across().start()
+                if s == 2:
+                    across().wait_recv()
+                    work[own] += mid[...]
+                    beside().start()
+                if s == 3:
+                    beside().wait_recv()
+                    done[own] = work[own] + side[...]
+                    back().start()
+                if s == 4:
+                    back().wait_recv()
+                    outward().start()
+                    store().start()
+                if s == 5:
+                    for copy in (across, beside, back, outward):
+                        copy().wait_send()
+                    store().wait()
+
+    def tick(self, t):
+        for s in reversed(range(STAGES)):
+            if 0 <= t - s < len(self.chunks):
+                self.stage(t - s, s)
+
+
+class SideFirst:
+    def __init__(self, peers, chunks, scratch):
+        self.p, self.chunks = peers, chunks
+        self.land, self.work, self.line, self.mid, self.done, self.sems, self.local = scratch
+
+    @staticmethod
+    def scratch():
+        return [pltpu.VMEM((SLOTS, CHUNK // 2, 1024), jnp.float32)] * 5 + [
+            pltpu.SemaphoreType.DMA((2, 5, SLOTS)),
+            pltpu.SemaphoreType.DMA((2, SLOTS)),
+        ]
+
+    def stage(self, c, s):
+        p, slot = self.p, c % SLOTS
+        part, total, row, cols = self.chunks[c]
+        lanes, half = pl.ds(0, cols), CHUNK // 2
+        own = pl.ds(pl.multiple_of(row + p.y_half * half, half), half)
+        other = pl.ds(pl.multiple_of(row + (1 - p.y_half) * half, half), half)
+        land, work = self.land.at[slot, :, lanes], self.work.at[slot, :, lanes]
+        line, mid = self.line.at[slot, :, lanes], self.mid.at[slot, :, lanes]
+        done = self.done.at[slot, :, lanes]
+        beside = functools.partial(remote, part.at[other], land, self.sems, (0, slot), p.y)
+        inward = functools.partial(remote, work, line, self.sems, (1, slot), p.z_pair)
+        across = functools.partial(remote, work, mid, self.sems, (2, slot), p.z_mid)
+        outward = functools.partial(remote, done, done, self.sems, (3, slot), p.z_pair)
+        back = functools.partial(remote, done, total.at[own], self.sems, (4, slot), p.y)
+        fetch = functools.partial(pltpu.make_async_copy, part.at[own], work, self.local.at[0, slot])
+        store = functools.partial(pltpu.make_async_copy, done, total.at[own], self.local.at[1, slot])
+
+        if s == 0:
+            beside().start()
+            fetch().start()
+        if s == 1:
+            fetch().wait()
+            beside().wait_recv()
+            work[...] += land[...]
+
+            @pl.when(p.end)
+            def _():
+                inward().start()
+
+        if s in (2, 3):
+
+            @pl.when(p.middle)
+            def _():
+                if s == 2:
+                    inward().wait_recv()
+                    work[...] += line[...]
+                    across().start()
+                if s == 3:
+                    across().wait_recv()
+                    done[...] = work[...] + mid[...]
+                    outward().start()
+
+        if s == 4:
+
+            @pl.when(p.end)
+            def _():
+                outward().wait_recv()
+
+            back().start()
+            store().start()
+        if s == 5:
+            back().wait()
+            beside().wait_send()
+            store().wait()
+
+            @pl.when(p.end)
+            def _():
+                inward().wait_send()
+
+            @pl.when(p.middle)
+            def _():
+                across().wait_send()
+                outward().wait_send()
+
+    def tick(self, t):
+        for s in reversed(range(STAGES)):
+            if 0 <= t - s < len(self.chunks):
+                self.stage(t - s, s)
+
+
+class SmallSum:
+    def __init__(self, peers, scratch):
+        self.p = peers
+        self.kept, self.got, self.sems = scratch
+
+    @staticmethod
+    def scratch():
+        return [
+            pltpu.VMEM((6, 8, 1024), jnp.float32),
+            pltpu.VMEM((5, 8, 1024), jnp.float32),
+            pltpu.SemaphoreType.DMA((2, 5)),
+        ]
+
+    def copy(self, s):
+        p = self.p
+        partner = (p.y, p.z_pair, p.z_far, p.core, p.x)[s]
+        return remote(self.kept.at[s], self.got.at[s], self.sems, (s,), partner)
+
+    def start(self, rows):
+        self.kept[0] = rows
+        self.copy(0).start()
+
+    def step(self, s):
+        self.copy(s).wait()
+        self.kept[s + 1] = self.kept[s] + self.got[s]
+        if s < 4:
+            self.copy(s + 1).start()
+
+
+def chunk_lists(parts, totals):
+    ways = ([], [])
+    for turn, (part, total) in enumerate(zip(parts, totals)):
+        for i in range(part.shape[0] // CHUNK):
+            ways[(turn if turn < 2 else i) % 2].append((part, total, i * CHUNK, part.shape[1]))
+    return ways
+
+
+def sums_kernel(dp_size, w_out, w_in, w_dense, w_qkv, small, *rest):
+    totals, small_total, scratch = rest[:4], rest[4], rest[5:]
+    peers = Peers(dp_size)
+    peers.greet()
+    line, side = chunk_lists((w_out, w_in, w_dense, w_qkv), totals)
+    first = LineFirst(peers, line, scratch[:7])
+    second = SideFirst(peers, side, scratch[7:14])
+    little = SmallSum(peers, scratch[14:])
+    little.start(small[...])
+    for t in range(max(len(line), len(side)) + STAGES - 1):
+        first.tick(t)
+        second.tick(t)
+        if t < 5:
+            little.step(t)
+            if t == 2:
+                small_total[0:8] = little.kept[3]
+            if t == 4:
+                small_total[8:16] = little.kept[5]
+
+
+def group_sums(dp_size, parts, small):
+    vm = pl.BlockSpec(memory_space=pltpu.VMEM)
+    hbm = pl.BlockSpec(memory_space=pl.ANY)
+    outs = [jax.ShapeDtypeStruct(p.shape, jnp.float32) for p in parts]
+    return pl.pallas_call(
+        functools.partial(sums_kernel, dp_size),
+        out_shape=tuple(outs) + (jax.ShapeDtypeStruct((16, 1024), jnp.float32),),
+        in_specs=[hbm] * 4 + [vm],
+        out_specs=tuple([hbm] * 4 + [vm]),
+        scratch_shapes=LineFirst.scratch() + SideFirst.scratch() + SmallSum.scratch(),
+        compiler_params=pltpu.CompilerParams(
+            collective_id=0, has_side_effects=True, vmem_limit_bytes=40 << 20
+        ),
+        name="group_sums",
+    )(*parts, small)
+
+
+def rest_groups(dp_size):
+    stride = z_stride(dp_size)
+    places = np.arange(dp_size).reshape(-1, 4, stride // 2, 2)
+    return places.transpose(1, 3, 0, 2).reshape(8, -1).tolist()
+
+
 def rotate(source, tables):
     tokens, width = source.shape
     cos_t, low_t, high_t = tables
@@ -312,6 +605,7 @@
 
 
 def on_device(
+    dp_size,
     layer_input,
     positions,
     block_ids,
@@ -381,27 +675,17 @@
     branches, d_full = lax.psum((branch, d_normed), "tensor")
     output = (input_float + branches + b_dense + b_out).astype(jnp.bfloat16)
     grad_input = norm_back(d_full, standard, inv_std, cot_float, ln_gain)
-    grad_gain, grad_shift = lax.psum((grad_ln[0], grad_ln[1]), ("dp", "tensor"))
-    (
-        grad_w_qkv,
-        grad_b_qkv,
-        grad_w_dense,
-        bias_grad,
-        grad_w_in,
-        grad_b_in,
-        grad_w_out,
-    ) = lax.psum(
-        (
-            grad_w_qkv,
-            grad_b_qkv[0],
-            grad_w_dense,
-            bias_grad,
-            grad_w_in,
-            grad_b_in,
-            grad_w_out,
-        ),
-        "dp",
-    )
+    pad = jnp.zeros((1024 - 3 * width,), jnp.float32)
+    small = jnp.stack(
+        [grad_ln[0], grad_ln[1], bias_grad, grad_b_in, jnp.concatenate([grad_b_qkv[0], pad])]
+        + [jnp.zeros((d,), jnp.float32)] * 3
+    )
+    sums = group_sums(dp_size, (grad_w_out, grad_w_in, grad_w_dense, grad_w_qkv), small)
+    if dp_size > 8:
+        sums = lax.psum(sums, "dp", axis_index_groups=rest_groups(dp_size))
+    grad_w_out, grad_w_in, grad_w_dense, grad_w_qkv, small = sums
+    bias_grad, grad_b_in, grad_b_qkv = small[2], small[3], small[4, : 3 * width]
+    grad_gain, grad_shift = small[8], small[9]
     return (
         output,
         grad_input,
@@ -450,5 +734,5 @@
         P(),
     )
     return jax.shard_map(
-        on_device, mesh=mesh, in_specs=in_specs, out_specs=out_specs, check_vma=False
-    )
+        functools.partial(on_device, mesh.shape["dp"]), mesh=mesh, in_specs=in_specs, out_specs=out_specs, check_vma=False
+    )

time: 966 us -> 808 us (0.84)
  waiting for transfers between devices: 578 us -> 274 us
  Pallas kernels: 104 us -> 337 us
  blocking collectives: 82.8 us -> 0 us
    psum x1 -> x0, waiting for transfers between devices: 346 us -> none  [on_device(): lax.psum((grad_w_qkv, grad_b_qkv[0], grad_w_dense, bias_grad, grad_w_in,...]
    pallas_call x0 -> x1, Pallas kernels: none -> 233 us  [group_sums(): pl.pallas_call(functools.partial(sums_kernel, dp_size), out_shape=tuple(o...]
    psum x2 -> x0, blocking collectives: 82.8 us -> none  [the longest x1 43.2 us: on_device(): grad_gain, grad_shift = lax.psum((grad_ln[0], grad_ln[1]), ('dp', 'tensor'))]
    psum x1, waiting for transfers between devices: 232 us -> 274 us  [on_device(): branches, d_full = lax.psum((branch, d_normed), 'tensor')]
  transfers between devices with their start and end apart: 2 -> 1, of which waited for: 2 -> 1; matrix products, arithmetic and copies ran while one was open for 4% -> 2% of each run, Pallas kernels for 0% -> 0%
where the time goes in v2:
time: 808 us; the launch traced here: 798 us
  Pallas kernels  337 us (42%)
  waiting for transfers between devices  274 us (34%)
  local copies, waits for them, and re-layouts  69.3 us (9%)
  matrix products  55.1 us (7%)
  other arithmetic  48.4 us (6%)
  between operations  14.6 us (2%)
    psum x1, waiting for transfers between devices, on_device(): branches, d_full = lax.psum((branch, d_normed), 'tensor')  274 us
    pallas_call x1, Pallas kernels, group_sums(): pl.pallas_call(functools.partial(sums_kernel, dp_size), out_shape=tuple(o...  233 us
    pallas_call x1, Pallas kernels, attention(): pl.pallas_call(functools.partial(attention_kernel, heads), out_shape=(jax...  104 us
    slice x4, local copies, waits for them, and re-layouts, rotate(): up = jnp.roll(pairs, -8, axis=2)  19 us
    unnamed x70, local copies, waits for them, and re-layouts  18.4 us
  transfers between devices with their start and end apart: 1, of which 1 were waited for; matrix products, arithmetic and copies ran while one was open for 2% of the time, Pallas kernels for 0%

profile of v2, /device:TPU:0, one launch (start us, length us, event | category | flops | bytes accessed | tf_op | source)
XLA Modules:
  0.0 798.3 jit_solution(14847805931079603389)
XLA Ops:
  7.2 0.0 all-reduce.4.cloned.1.call-start
  7.3 3.0 convert_reduce_fusion
  10.2 0.6 copy-done.4
  10.8 1.4 fusion.10
  12.3 2.6 copy.35
  14.8 2.4 fusion.29
  17.2 0.1 reshape.123
  17.3 0.1 add.124
  17.4 3.3 fusion.6.normed
  20.7 2.0 copy-done.11
  22.7 2.7 convolution_add_fusion.1
  25.4 3.2 reshape.125
  28.6 5.8 fusion.25
  34.4 3.6 fusion.26
  38.1 0.1 add.119
  38.2 4.8 convolution_add_fusion.2
  43.0 3.2 reshape.124
  46.3 5.8 fusion.27
  52.1 3.7 fusion.28
  55.8 5.5 multiply_cosine_fusion
  61.3 1.0 broadcast_in_dim.11
  62.4 1.0 broadcast_in_dim.12
  63.4 5.6 concatenate.34.low_t
  69.0 5.5 concatenate.36.high_t
  74.5 0.1 add.129
  74.6 7.5 multiply_convert_fusion
  82.1 7.8 convert_reduce_fusion.2
  90.0 7.0 fusion.32.dn_hbm
  97.0 6.7 fusion.31.mlp_hbm
  103.7 1.4 copy.41.inv_std
  105.0 1.3 copy.40.row_mean
  106.4 1.4 copy.39.ids_col
  107.8 0.1 broadcast_in_dim.10
  107.8 2.2 concatenate.32.cos_t
  110.1 11.8 %maximum_multiply_fusion.2 = (f32[2048,2,128]{2,1,0:T(2,128)S(1)}, f32[2048,2,128]{2,1,0:T(2,128)S(1)}, f32[2048,2,128]{2,1,0:T(2,128)S(1)}, f32[2048,2,128]{2,1,0:T(2,128)S(1)}) fusion(f32[2048,2,8]{2,1,0:T(2,128)} %get-tuple-element.46, f32[2048,2,120]{2,1,0:T(2,128)} %get-tuple-element.44, f32[2048,128]{1,0:T(8,128)} %concatenate.34.low_t, ...), kind=kLoop, calls=%fused_computation.44 | loop fusion | flops 4194304 | bytes 18874368 | tf_op jit(solution)/shard_map/mul | solution.py:593
  121.9 1.2 mul.175
  123.0 0.4 copy-done.14
  123.4 1.6 fusion.21.k
  125.0 0.3 copy-done.15
  125.3 1.6 fusion.23.q
  126.9 0.9 copy-done.12
  127.9 0.1 copy-done.17
  128.0 2.3 fusion.20.v
  130.3 103.9 %attention.1 = (f32[2048,1024]{1,0:T(8,128)}, f32[2048,1024]{1,0:T(8,128)}, f32[256,1024]{1,0:T(8,128)}, f32[1024,768]{1,0:T(8,128)}, f32[1,768]{1,0:T(1,128)}, /*index=5*/f32[8,1024]{1,0:T(8,128)}) custom-call(bf16[2048,256]{1,0:T(8,128)(2,1)} %fusion.23.q, bf16[2048,256]{1,0:T(8,128)(2,1)} %fusion.21.k, bf16[2048,256]{1,0:T(8,128)(2,1)} %fusion.20.v, ...), custom_call_target="tpu_custom_call" | custom-call | tf_op jit(solution)/shard_map/attention/pallas_call | solution.py:259
  234.2 0.0 all-reduce.4.cloned.1.call-update
  234.2 0.7 copy-done.26
  234.9 0.8 slice.86
  235.7 10.2 %fusion.34.w_in = f32[1024,1024]{1,0:T(8,128)} fusion(bf16[2048,1024]{1,0:T(8,128)(2,1)} %copy-done.11, bf16[2048,1024]{1,0:T(8,128)(2,1)} %copy-done.31), kind=kOutput, calls=%fused_computation.68 | convolution fusion | flops 4294967296 | bytes 12582912 | tf_op jit(solution)/shard_map/td,tf->df/dot_general | solution.py:655
  245.9 6.1 fusion.33.w_out
  251.9 274.0 %all-reduce.4.cloned.1.call-done = (f32[2048,1024]{1,0:T(8,128)}, f32[2048,1024]{1,0:T(8,128)}) async-done(((f32[2048,1024]{1,0:T(8,128)}, f32[2048,1024]{1,0:T(8,128)}), (f32[2048,1024]{1,0:T(8,128)}, f32[2048,1024]{1,0:T(8,128)})) %all-reduce.4.cloned.1.call-update) | async-done | bytes 16777232 | tf_op jit(solution)/shard_map/psum | solution.py:675
  525.9 7.3 multiply_reduce_fusion
  533.2 1.0 copy-done.8
  534.2 13.0 %convert_reduce_fusion.1 = (f32[1024]{0:T(1024)S(1)}, f32[2048,1024]{1,0:T(8,128)}, bf16[2048,1024]{1,0:T(8,128)(2,1)}) fusion(bf16[2048,1024]{1,0:T(8,128)(2,1)} %cot.1, f32[2048]{0:T(1024)S(1)} %broadcast_multiply_fusion, f32[2048]{0:T(1024)S(1)} %broadcast_multiply_fusion.2, bf16[2048,1024]{1,0:T(8,128)(2,1)S(1)} %copy-done.5, ...), kind=kLoop, calls=%fused_computation.4 | loop fusion | flops 31456256 | bytes 37797888 | tf_op jit(solution)/shard_map/reduce_sum | solution.py:650
  547.2 0.1 stack.19.small
  547.3 1.2 copy-done.3
  548.5 233.1 %group_sums.1 = (f32[1024,1024]{1,0:T(8,128)S(1)}, f32[1024,1024]{1,0:T(8,128)}, f32[256,1024]{1,0:T(8,128)S(1)}, f32[1024,768]{1,0:T(8,128)S(1)}, f32[16,1024]{1,0:T(8,128)S(1)}) custom-call(f32[1024,1024]{1,0:T(8,128)} %fusion.33.w_out, f32[1024,1024]{1,0:T(8,128)} %fusion.34.w_in, f32[256,1024]{1,0:T(8,128)S(1)} %copy-done.3, f32[1024,768]{1,0:T(8,128)S(1)} %copy-done.2, ...), custom_call_target="tpu_custom_call" | custom-call | tf_op jit(solution)/shard_map/group_sums/pallas_call | solution.py:568
  781.6 0.6 fusion.30
  782.2 0.6 slice_reduce_fusion
  782.8 0.6 copy.68
  783.4 1.7 copy.69
  785.1 1.0 copy.70
  786.0 1.1 copy-done.16
  787.1 2.1 copy.71
  789.2 2.0 copy.72
  (65 shorter events, 0.2 us)
Async XLA Ops:
  7.2 67.4 %copy-start = (bf16[1024,1024]{1,0:T(8,128)(2,1)S(1)}, bf16[1024,1024]{1,0:T(8,128)(2,1)}, u32[]{:S(2)}) copy-start(bf16[1024,1024]{1,0:T(8,128)(2,1)} %param.24) | copy-start | bytes 6291460
  7.2 518.7 %all-reduce.4.cloned.1.call-start = ((), (), s32[]{:S(2)}) async-start(), calls=%async_computation | async-start | bytes 33554432 | tf_op jit(solution)/shard_map/psum | solution.py:675
  7.2 3.6 copy-start.4
  12.2 5.0 copy-start.25
  12.2 5.2 copy-start.18
  12.2 5.2 copy-start.22
  20.7 2.0 copy-start.11
  28.6 5.8 copy-start.6
  46.2 5.8 copy-start.7
  52.1 3.7 copy-start.21
  69.0 5.6 copy-start.28
  74.6 7.5 copy-start.9
  74.6 7.5 copy-start.27
  82.1 14.9 %copy-start.29 = (bf16[2048,1024]{1,0:T(8,128)(2,1)}, bf16[2048,1024]{1,0:T(8,128)(2,1)S(1)}, u32[]{:S(2)}) copy-start(bf16[2048,1024]{1,0:T(8,128)(2,1)S(1)} %get-tuple-element.66) | copy-start | bytes 12582916
  90.0 7.0 copy-start.31
  97.0 9.4 %copy-start.19 = (s32[2048]{0:T(1024)S(1)}, s32[2048]{0:T(1024)}, u32[]{:S(2)}) copy-start(s32[2048]{0:T(1024)} %param.17) | copy-start | bytes 24580
  110.1 11.8 %copy-start.13 = (f32[2048,128]{1,0:T(8,128)}, f32[2048,128]{1,0:T(8,128)S(1)}, u32[]{:S(2)}) copy-start(f32[2048,128]{1,0:T(8,128)S(1)} %concatenate.32.cos_t) | copy-start | bytes 3145732
  121.8 1.6 copy-start.14
  123.4 1.9 copy-start.15
  125.3 2.6 copy-start.12
  125.3 2.7 copy-start.17
  234.2 0.7 copy-start.26
  235.6 10.2 %copy-start.10 = (bf16[2048,1024]{1,0:T(8,128)(2,1)S(1)}, bf16[2048,1024]{1,0:T(8,128)(2,1)}, u32[]{:S(2)}) copy-start(bf16[2048,1024]{1,0:T(8,128)(2,1)} %cot.1) | copy-start | bytes 12582916
  235.6 10.2 %copy-start.30 = (bf16[2048,1024]{1,0:T(8,128)(2,1)S(1)}, bf16[2048,1024]{1,0:T(8,128)(2,1)}, u32[]{:S(2)}) copy-start(bf16[2048,1024]{1,0:T(8,128)(2,1)} %copy-done.29) | copy-start | bytes 12582916
  525.9 7.3 copy-start.5
  525.9 8.3 %copy-start.8 = (f32[2048,1024]{1,0:T(8,128)S(1)}, f32[2048,1024]{1,0:T(8,128)}, u32[]{:S(2)}) copy-start(f32[2048,1024]{1,0:T(8,128)} %get-tuple-element.40) | copy-start | bytes 25165828
  525.9 8.3 %copy-start.23 = (f32[1024]{0:T(1024)S(1)}, f32[1024]{0:T(1024)}, u32[]{:S(2)}) copy-start(f32[1024]{0:T(1024)} %param.27) | copy-start | bytes 12292
  525.9 8.3 %copy-start.24 = (f32[1024]{0:T(1024)S(1)}, f32[1024]{0:T(1024)}, u32[]{:S(2)}) copy-start(f32[1024]{0:T(1024)} %param.23) | copy-start | bytes 12292
  534.2 13.0 %copy-start.2 = (f32[1024,768]{1,0:T(8,128)S(1)}, f32[1024,768]{1,0:T(8,128)}, u32[]{:S(2)}) copy-start(f32[1024,768]{1,0:T(8,128)} %get-tuple-element.26.w_qkv) | copy-start | bytes 9437188
  547.3 1.2 copy-start.3
  782.2 3.8 copy-start.20
  783.4 3.7 copy-start.16
  787.1 4.2 copy-start.1
Sparse Core Ops, SparseCore 0:
  234.3 291.5 all-reduce.3
